TPU v7x, 256 devices: a whole 4x4x8 slice. The times are simulated.
256 devices in a mesh: segment: 4 (over y), mp: 16 (over z, core), dp: 4 (over x).
Axes of the slice: x: 4, y: 4, z: 8, core: 2. Of those that a mesh axis runs over, the one named last changes fastest.
Arguments:
- text_rows: bfloat16 [4, 512, 1024], P(None, 'dp'), may hold values from -6 to 6
- durations: int32 [4, 4, 128], P(None, 'dp'), may hold values from 1 to 16, 512 in all within a row
- unit_targets: int32 [4, 2048], P(None, 'dp'), may hold values from 0 to 9999
- w_in: bfloat16 [4, 1024, 8192], P('segment', None, 'mp'), may hold values from -0.1875 to 0.1875
- w_out: bfloat16 [4, 8192, 1024], P('segment', 'mp'), may hold values from -0.0625 to 0.0625
- w_unit: bfloat16 [1024, 10240], P(None, ('segment', 'mp')), as said below
Outputs:
- loss: float32 [4], P('dp')
- grad_in: float32 [4, 1024, 8192], P('segment', 'dp', 'mp')
- grad_out: float32 [4, 8192, 1024], P('segment', 'mp', 'dp')
- grad_unit: float32 [1024, 10240], P('dp', ('segment', 'mp'))
Inputs may be any that keep to these rules, and one draw needn't show every extreme that they name: Within each micro-batch and each index of dp the 128 durations sum to exactly 512, and one of them equals 16. `w_unit`: entries of order 3 / sqrt(1024) in most columns, some columns much larger.
All inputs are finite; a program needn't handle non-finite values.
Results may differ from a plain program's by a relative error of at most 0.035.
Values may be sent and summed in bfloat16 or wider, within the bound.
A program may use at most 128 MiB of HBM per device.

v0:
```python
import jax
import jax.numpy as jnp
from jax import lax
from jax.sharding import PartitionSpec as P


def shifted(block, axis, distance):
    devices = range(lax.axis_size(axis))
    route = [(i - distance, i) for i in devices if i - distance in devices]
    return lax.ppermute(block, axis, route)


def broadcast(x, axis, root):
    mine = lax.axis_index(axis) == root
    return lax.psum(jnp.where(mine, x, jnp.zeros_like(x)), axis)


def gelu_parts(pre_vals):
    coeff = 0.7978845608
    inner = coeff * (pre_vals + 0.044715 * pre_vals * pre_vals * pre_vals)
    tanh_val = jnp.tanh(inner)
    value = 0.5 * pre_vals * (1.0 + tanh_val)
    slope = 0.5 * (1.0 + tanh_val) + 0.5 * pre_vals * (1.0 - tanh_val * tanh_val) * coeff * (
        1.0 + 3.0 * 0.044715 * pre_vals * pre_vals
    )
    return (value, slope)


def row_scale(rows_in):
    floats = rows_in.astype(jnp.float32)
    return lax.rsqrt(jnp.mean(floats * floats, axis=-1, keepdims=True) + 1e-06)


def norm_back(rows_in, grads):
    scale = row_scale(rows_in)
    normal = rows_in.astype(jnp.float32) * scale
    return scale * (grads - normal * jnp.mean(grads * normal, axis=-1, keepdims=True))


def section(rows_in, first):
    normed = (rows_in.astype(jnp.float32) * row_scale(rows_in)).astype(jnp.bfloat16)
    pre_vals = jnp.dot(normed, first, preferred_element_type=jnp.float32)
    value, slope = gelu_parts(pre_vals)
    return (normed, value.astype(jnp.bfloat16), slope)


def finish_forward(pieces, summed):
    return (pieces[0].astype(jnp.float32) + summed).astype(jnp.bfloat16)


def finish_backward(pieces, summed):
    return (pieces[0].astype(jnp.float32) + norm_back(pieces[1], summed)).astype(jnp.bfloat16)


def reduce_rows(partial_value, pieces, finisher):
    summed = lax.psum(partial_value, "mp")
    return finisher(pieces, summed)


def on_device(text_rows, durations, unit_targets, w_in, w_out, w_unit):
    micro_count, row_count, width = text_rows.shape
    segments = lax.axis_size("segment")
    segment_at = lax.axis_index("segment")
    first = w_in[0]
    second = w_out[0]
    clocks = micro_count + segments - 1
    stash = jnp.zeros((micro_count, row_count, width), jnp.bfloat16)
    final_rows = jnp.zeros((micro_count, row_count, width), jnp.bfloat16)
    outgoing = jnp.zeros((row_count, width), jnp.bfloat16)
    for clock in range(clocks):
        if clock > 0:
            incoming = shifted(outgoing, "segment", 1)
        else:
            incoming = jnp.zeros((row_count, width), jnp.bfloat16)
        rows_in = jnp.where(segment_at == 0, text_rows[min(clock, micro_count - 1)], incoming)
        batch_at = clock - segment_at
        is_live = (batch_at >= 0) & (batch_at < micro_count)
        slot_at = jnp.clip(batch_at, 0, micro_count - 1)
        stash = jnp.where(
            is_live, lax.dynamic_update_index_in_dim(stash, rows_in, slot_at, 0), stash
        )
        normed, hidden, slope = section(rows_in, first)
        partial_value = jnp.dot(hidden, second, preferred_element_type=jnp.float32)
        outgoing = reduce_rows(partial_value, (rows_in,), finish_forward)
        is_last = is_live & (segment_at == segments - 1)
        final_rows = jnp.where(
            is_last, lax.dynamic_update_index_in_dim(final_rows, outgoing, slot_at, 0), final_rows
        )
    final_rows = broadcast(final_rows, "segment", segments - 1)
    vocab_part = w_unit.shape[1]
    vocab_start = lax.axis_index(("segment", "mp")) * vocab_part
    final_norm = (final_rows.astype(jnp.float32) * row_scale(final_rows)).astype(jnp.bfloat16)
    logits = jnp.einsum("mrd,dv->mrv", final_norm, w_unit, preferred_element_type=jnp.float32)
    lengths = durations[:, 0, :]
    unit_count = unit_targets.shape[1]
    ends = jnp.cumsum(lengths, axis=-1)
    positions = jnp.arange(unit_count, dtype=jnp.int32)
    row_local = jnp.sum((ends[:, None, :] <= positions[None, :, None]).astype(jnp.int32), axis=-1)
    row_onehot = (
        row_local[:, :, None] == jnp.arange(row_count, dtype=jnp.int32)[None, None, :]
    ).astype(jnp.bfloat16)
    vocab_ids = vocab_start + jnp.arange(vocab_part, dtype=jnp.int32)
    target_hits = (unit_targets[:, :, None] == vocab_ids[None, None, :]).astype(jnp.bfloat16)
    counts = jnp.einsum("mur,muv->mrv", row_onehot, target_hits, preferred_element_type=jnp.float32)
    local_peak = jnp.max(logits, axis=-1)
    target_local = jnp.sum(counts * logits, axis=-1)
    peak = lax.pmax(local_peak, ("segment", "mp"))
    total, target_sum = lax.psum(
        (jnp.sum(jnp.exp(logits - peak[..., None]), axis=-1), target_local), ("segment", "mp")
    )
    lse = peak + jnp.log(total)
    denom = float(micro_count * unit_count * lax.axis_size("dp"))
    length_f = lengths.astype(jnp.float32)
    loss_local = jnp.sum(length_f * lse - target_sum)
    loss = (loss_local / denom)[None]
    dlogits = ((length_f[..., None] * jnp.exp(logits - lse[..., None]) - counts) / denom).astype(
        jnp.bfloat16
    )
    grad_unit = jnp.einsum("mrd,mrv->dv", final_norm, dlogits, preferred_element_type=jnp.float32)
    norm_part = jnp.einsum("mrv,dv->mrd", dlogits, w_unit, preferred_element_type=jnp.float32)
    norm_share = lax.psum_scatter(
        norm_part, ("segment", "mp"), scatter_dimension=2, tiled=True
    ).astype(jnp.bfloat16)
    dnorm = lax.all_gather(norm_share, ("segment", "mp"), axis=2, tiled=True)
    grad_final = norm_back(final_rows, dnorm.astype(jnp.float32)).astype(jnp.bfloat16)
    grad_first = jnp.zeros(first.shape, jnp.float32)
    grad_second = jnp.zeros(second.shape, jnp.float32)
    going_back = jnp.zeros((row_count, width), jnp.bfloat16)
    for clock in range(clocks):
        if clock > 0:
            arriving = shifted(going_back, "segment", -1)
        else:
            arriving = jnp.zeros((row_count, width), jnp.bfloat16)
        grad_rows = jnp.where(
            segment_at == segments - 1, grad_final[min(clock, micro_count - 1)], arriving
        )
        batch_at = clock - (segments - 1 - segment_at)
        is_live = (batch_at >= 0) & (batch_at < micro_count)
        slot_at = jnp.clip(batch_at, 0, micro_count - 1)
        rows_in = lax.dynamic_index_in_dim(stash, slot_at, 0, keepdims=False)
        normed, hidden, slope = section(rows_in, first)
        live_f = is_live.astype(jnp.float32)
        grad_second = grad_second + live_f * jnp.dot(
            hidden.T, grad_rows, preferred_element_type=jnp.float32
        )
        dhidden = jnp.dot(grad_rows, second.T, preferred_element_type=jnp.float32)
        dpre = (dhidden * slope).astype(jnp.bfloat16)
        grad_first = grad_first + live_f * jnp.dot(
            normed.T, dpre, preferred_element_type=jnp.float32
        )
        dnormed = jnp.dot(dpre, first.T, preferred_element_type=jnp.float32)
        going_back = reduce_rows(dnormed, (grad_rows, rows_in), finish_backward)
    sum_first, sum_second, sum_unit = (
        lax.psum_scatter(grad_first, "dp", scatter_dimension=0, tiled=True),
        lax.psum_scatter(grad_second, "dp", scatter_dimension=1, tiled=True),
        lax.psum_scatter(grad_unit, "dp", scatter_dimension=0, tiled=True),
    )
    return (loss, sum_first[None], sum_second[None], sum_unit)


def solution(mesh):
    placed = (
        P(None, "dp", None),
        P(None, "dp", None),
        P(None, "dp"),
        P("segment", None, "mp"),
        P("segment", "mp", None),
        P(None, ("segment", "mp")),
    )
    return jax.shard_map(
        on_device,
        mesh=mesh,
        in_specs=placed,
        out_specs=(
            P("dp"),
            P("segment", "dp", "mp"),
            P("segment", "mp", "dp"),
            P("dp", ("segment", "mp")),
        ),
        check_vma=False,
    )
```

profile of v0, /device:TPU:1, one launch (start us, length us, event | category | flops | bytes accessed | tf_op | source)
XLA Modules:
  0.0 2379.7 jit_solution(6565013018614124377)
XLA Ops:
  11.3 113.5 %all-reduce.18.cloned.1.call-done = f32[128,1024]{1,0:T(8,128)} async-done(((f32[128,1024]{1,0:T(8,128)}), f32[128,1024]{1,0:T(8,128)}) %all-reduce.18.cloned.1.call-update) | async-done | bytes 524304 | tf_op jit(solution)/shard_map/psum | solution.py:56
  137.0 111.0 %all-reduce.20.cloned.1.call-done = f32[128,1024]{1,0:T(8,128)} async-done(((f32[128,1024]{1,0:T(8,128)}), f32[128,1024]{1,0:T(8,128)}) %all-reduce.20.cloned.1.call-update) | async-done | bytes 524304 | tf_op jit(solution)/shard_map/psum | solution.py:56
  253.2 5.2 collective-permute-done.1
  261.9 110.8 %all-reduce.22.cloned.1.call-done = f32[128,1024]{1,0:T(8,128)} async-done(((f32[128,1024]{1,0:T(8,128)}), f32[128,1024]{1,0:T(8,128)}) %all-reduce.22.cloned.1.call-update) | async-done | bytes 524304 | tf_op jit(solution)/shard_map/psum | solution.py:56
  377.8 5.2 collective-permute-done.2
  386.5 110.8 %all-reduce.24.cloned.1.call-done = f32[128,1024]{1,0:T(8,128)} async-done(((f32[128,1024]{1,0:T(8,128)}), f32[128,1024]{1,0:T(8,128)}) %all-reduce.24.cloned.1.call-update) | async-done | bytes 524304 | tf_op jit(solution)/shard_map/psum | solution.py:56
  502.4 5.2 collective-permute-done.3
  511.1 110.8 %all-reduce.26.cloned.1.call-done = f32[128,1024]{1,0:T(8,128)} async-done(((f32[128,1024]{1,0:T(8,128)}), f32[128,1024]{1,0:T(8,128)}) %all-reduce.26.cloned.1.call-update) | async-done | bytes 524304 | tf_op jit(solution)/shard_map/psum | solution.py:56
  627.0 5.2 collective-permute-done.4
  635.7 110.8 %all-reduce.28.cloned.1.call-done = f32[128,1024]{1,0:T(8,128)} async-done(((f32[128,1024]{1,0:T(8,128)}), f32[128,1024]{1,0:T(8,128)}) %all-reduce.28.cloned.1.call-update) | async-done | bytes 524304 | tf_op jit(solution)/shard_map/psum | solution.py:56
  760.3 110.8 %all-reduce.30.cloned.1.call-done = f32[128,1024]{1,0:T(8,128)} async-done(((f32[128,1024]{1,0:T(8,128)}), f32[128,1024]{1,0:T(8,128)}) %all-reduce.30.cloned.1.call-update) | async-done | bytes 524304 | tf_op jit(solution)/shard_map/psum | solution.py:56
  876.2 49.1 %all-reduce.32.cloned.1.call-done = bf16[4,128,1024]{2,1,0:T(8,128)(2,1)} async-done(((bf16[4,128,1024]{2,1,0:T(8,128)(2,1)}), bf16[4,128,1024]{2,1,0:T(8,128)(2,1)}) %all-reduce.32.cloned.1.call-update) | async-done | bytes 1048592 | tf_op jit(solution)/shard_map/psum | solution.py:15
  929.3 125.5 %pmax.7 = f32[4,128]{1,0:T(4,128)S(1)} all-reduce(f32[4,128]{1,0:T(4,128)S(1)} %get-tuple-element.40), channel_id=1, replica_groups=mesh['segment'=4,'mp'=16,'dp'=4] {'segment','mp'}, use_global_device_ids=true, to_apply=%region_17.18 | all-reduce | flops 512 | bytes 4096 | tf_op jit(solution)/shard_map/pmax | solution.py:107
  1057.1 127.1 %psum.120 = f32[4,128]{1,0:T(4,128)S(1)} all-reduce(f32[4,128]{1,0:T(4,128)S(1)} %get-tuple-element.12), channel_id=1, replica_groups=mesh['segment'=4,'mp'=16,'dp'=4] {'segment','mp'}, use_global_device_ids=true, to_apply=%region_19.20 | all-reduce | flops 512 | bytes 4096 | tf_op jit(solution)/shard_map/psum | solution.py:108
  1189.2 265.5 %all-reduce.45 = (f32[4,128]{1,0:T(4,128)}, bf16[4,128,1024]{1,0,2:T(4,128)(2,1)}) all-reduce(f32[4,128]{1,0:T(4,128)S(1)} %get-tuple-element.13, f32[4,128,1024]{1,0,2:T(4,128)} %copy.13), channel_id=1, replica_groups=mesh['segment'=4,'mp'=16,'dp'=4] {'segment','mp'}, use_global_device_ids=true, to_apply=%region_23.24 | all-reduce | flops 524800 | bytes 3149824 | tf_op jit(solution)/shard_map/psum | solution.py:108
  1456.9 75.1 %all-gather.2.cloned.1.call-done = bf16[4,128,1024]{1,0,2:T(4,128)(2,1)} async-done(((bf16[4,128,16]{1,0,2:T(4,128)(2,1)}), bf16[4,128,1024]{1,0,2:T(4,128)(2,1)}) %all-gather.2.cloned.1.call-update) | async-done | bytes 1048592 | tf_op jit(solution)/shard_map/all_gather | solution.py:124
  1540.1 106.9 %all-reduce.34.cloned.1.call-done = f32[128,1024]{1,0:T(8,128)} async-done(((f32[128,1024]{1,0:T(8,128)}), f32[128,1024]{1,0:T(8,128)}) %all-reduce.34.cloned.1.call-update) | async-done | bytes 524304 | tf_op jit(solution)/shard_map/psum | solution.py:56
  1651.1 7.3 collective-permute-done.6
  1661.0 109.8 %all-reduce.36.cloned.1.call-done = f32[128,1024]{1,0:T(8,128)} async-done(((f32[128,1024]{1,0:T(8,128)}), f32[128,1024]{1,0:T(8,128)}) %all-reduce.36.cloned.1.call-update) | async-done | bytes 524304 | tf_op jit(solution)/shard_map/psum | solution.py:56
  1775.8 6.7 collective-permute-done.7
  1786.7 109.8 %all-reduce.38.cloned.1.call-done = f32[128,1024]{1,0:T(8,128)} async-done(((f32[128,1024]{1,0:T(8,128)}), f32[128,1024]{1,0:T(8,128)}) %all-reduce.38.cloned.1.call-update) | async-done | bytes 524304 | tf_op jit(solution)/shard_map/psum | solution.py:56
  1901.5 6.7 collective-permute-done.8
  1912.4 109.8 %all-reduce.40.cloned.1.call-done = f32[128,1024]{1,0:T(8,128)} async-done(((f32[128,1024]{1,0:T(8,128)}), f32[128,1024]{1,0:T(8,128)}) %all-reduce.40.cloned.1.call-update) | async-done | bytes 524304 | tf_op jit(solution)/shard_map/psum | solution.py:56
  2027.3 6.7 collective-permute-done.9
  2038.2 109.8 %all-reduce.42.cloned.1.call-done = f32[128,1024]{1,0:T(8,128)} async-done(((f32[128,1024]{1,0:T(8,128)}), f32[128,1024]{1,0:T(8,128)}) %all-reduce.42.cloned.1.call-update) | async-done | bytes 524304 | tf_op jit(solution)/shard_map/psum | solution.py:56
  2153.0 6.7 collective-permute-done.10
  2178.9 94.8 %all-reduce.44.cloned.1.call-done = f32[128,1024]{1,0:T(8,128)} async-done(((f32[128,1024]{1,0:T(8,128)}), f32[128,1024]{1,0:T(8,128)}) %all-reduce.44.cloned.1.call-update) | async-done | bytes 524304 | tf_op jit(solution)/shard_map/psum | solution.py:56
  2278.2 7.3 collective-permute-done.11
  2286.2 6.7 multiply_add_fusion
  2305.0 7.7 multiply_add_fusion.1
  2314.6 21.9 reduce-scatter.6.cloned.1.call-done
  2336.6 35.2 %reduce-scatter.4.cloned.1.call-done = f32[256,512]{1,0:T(8,128)} async-done(((f32[1024,512]{1,0:T(8,128)}), f32[256,512]{1,0:T(8,128)}) %reduce-scatter.4.cloned.1.call-update) | async-done | bytes 524304 | tf_op jit(solution)/shard_map/reduce_scatter | solution.py:154
  (293 shorter events, 166.7 us)
Async XLA Ops:
  7.2 117.6 %all-reduce.18.cloned.1.call-start = ((), (), s32[]{:S(2)}) async-start(), calls=%async_computation.3 | async-start | bytes 1048576 | tf_op jit(solution)/shard_map/psum | solution.py:56
  11.2 236.8 %all-reduce.20.cloned.1.call-start = ((), (), s32[]{:S(2)}) async-start(), calls=%async_computation.4 | async-start | bytes 1048576 | tf_op jit(solution)/shard_map/psum | solution.py:56
  126.2 8.0 collective-permute-start
  137.0 235.7 %all-reduce.22.cloned.1.call-start = ((), (), s32[]{:S(2)}) async-start(), calls=%async_computation.5 | async-start | bytes 1048576 | tf_op jit(solution)/shard_map/psum | solution.py:56
  250.1 8.3 collective-permute-start.1
  261.8 235.4 %all-reduce.24.cloned.1.call-start = ((), (), s32[]{:S(2)}) async-start(), calls=%async_computation.6 | async-start | bytes 1048576 | tf_op jit(solution)/shard_map/psum | solution.py:56
  374.7 8.3 collective-permute-start.2
  386.4 235.4 %all-reduce.26.cloned.1.call-start = ((), (), s32[]{:S(2)}) async-start(), calls=%async_computation.7 | async-start | bytes 1048576 | tf_op jit(solution)/shard_map/psum | solution.py:56
  499.3 8.3 collective-permute-start.3
  511.0 235.4 %all-reduce.28.cloned.1.call-start = ((), (), s32[]{:S(2)}) async-start(), calls=%async_computation.8 | async-start | bytes 1048576 | tf_op jit(solution)/shard_map/psum | solution.py:56
  623.9 8.3 collective-permute-start.4
  635.7 235.4 %all-reduce.30.cloned.1.call-start = ((), (), s32[]{:S(2)}) async-start(), calls=%async_computation.9 | async-start | bytes 1048576 | tf_op jit(solution)/shard_map/psum | solution.py:56
  748.5 8.3 collective-permute-start.5
  760.3 165.0 %all-reduce.32.cloned.1.call-start = ((), (), s32[]{:S(2)}) async-start(), calls=%async_computation.10 | async-start | bytes 2097152 | tf_op jit(solution)/shard_map/psum | solution.py:15
  874.2 180.6 %copy-start.59 = (s32[4,512]{1,0:T(4,128)S(1)}, s32[4,512]{1,0:T(4,128)}, u32[]{:S(2)}) copy-start(s32[4,512]{1,0:T(4,128)} %param.8) | copy-start | bytes 24580
  874.2 657.7 %all-gather.2.cloned.1.call-start = ((), (), s32[]{:S(2)}) async-start(), calls=%async_computation.11 | async-start | bytes 1064960 | tf_op jit(solution)/shard_map/all_gather | solution.py:124
  1456.1 190.9 %all-reduce.34.cloned.1.call-start = ((), (), s32[]{:S(2)}) async-start(), calls=%async_computation.12 | async-start | bytes 1048576 | tf_op jit(solution)/shard_map/psum | solution.py:56
  1456.5 192.7 %copy-start.55 = (f32[128]{0:T(128)}, f32[128]{0:T(128)S(1)}, u32[]{:S(2)}) copy-start(f32[128]{0:T(128)S(1)} %add_rsqrt_fusion.7) | copy-start | bytes 1540
  1540.0 230.8 %all-reduce.36.cloned.1.call-start = ((), (), s32[]{:S(2)}) async-start(), calls=%async_computation.13 | async-start | bytes 1048576 | tf_op jit(solution)/shard_map/psum | solution.py:56
  1649.4 9.0 collective-permute-start.6
  1661.0 235.5 %all-reduce.38.cloned.1.call-start = ((), (), s32[]{:S(2)}) async-start(), calls=%async_computation.14 | async-start | bytes 1048576 | tf_op jit(solution)/shard_map/psum | solution.py:56
  1773.4 9.0 collective-permute-start.7
  1786.6 235.6 %all-reduce.40.cloned.1.call-start = ((), (), s32[]{:S(2)}) async-start(), calls=%async_computation.15 | async-start | bytes 1048576 | tf_op jit(solution)/shard_map/psum | solution.py:56
  1899.1 9.0 collective-permute-start.8
  1912.4 235.6 %all-reduce.42.cloned.1.call-start = ((), (), s32[]{:S(2)}) async-start(), calls=%async_computation.16 | async-start | bytes 1048576 | tf_op jit(solution)/shard_map/psum | solution.py:56
  2024.9 9.0 collective-permute-start.9
  2038.1 235.6 %all-reduce.44.cloned.1.call-start = ((), (), s32[]{:S(2)}) async-start(), calls=%async_computation.17 | async-start | bytes 1048576 | tf_op jit(solution)/shard_map/psum | solution.py:56
  2150.7 9.0 collective-permute-start.10
  2163.9 150.7 %reduce-scatter.8.cloned.1.call-start = ((), (), s32[]{:S(2)}) async-start(), calls=%async_computation.20 | async-start | bytes 819200 | tf_op jit(solution)/shard_map/reduce_scatter | solution.py:156
  2166.6 169.9 %reduce-scatter.6.cloned.1.call-start = ((), (), s32[]{:S(2)}) async-start(), calls=%async_computation.19 | async-start | bytes 2621440 | tf_op jit(solution)/shard_map/reduce_scatter | solution.py:155
  2276.5 9.0 collective-permute-start.11
  2292.9 78.8 %reduce-scatter.4.cloned.1.call-start = ((), (), s32[]{:S(2)}) async-start(), calls=%async_computation.18 | async-start | bytes 2621440 | tf_op jit(solution)/shard_map/reduce_scatter | solution.py:154
  (59 other events, 808.3 us)
Sparse Core Ops, SparseCore 0:
  11.4 113.3 all-reduce.17
  137.1 110.8 all-reduce.19
  261.9 110.6 all-reduce.21
  386.5 110.6 all-reduce.23
  511.2 110.6 all-reduce.25
  635.8 110.6 all-reduce.27
  760.4 110.6 all-reduce.29
  874.3 50.9 all-reduce.31
  1456.2 75.6 all-gather.1
  1540.1 106.8 all-reduce.33
  1661.1 109.7 all-reduce.35
  1786.8 109.7 all-reduce.37
  1912.5 109.7 all-reduce.39
  2038.3 109.7 all-reduce.41
  2164.0 109.6 all-reduce.43
  2276.7 23.4 reduce-scatter.7
  2303.2 33.2 reduce-scatter.5
  2339.7 31.9 reduce-scatter.3
where the time goes:
time: 2380 us
  waiting for transfers between devices  1670 us (70%)
  blocking collectives  518 us (22%)
  matrix products  70.9 us (3%)
  other arithmetic  53.3 us (2%)
  starting transfers between devices  28.3 us (1%)
    psum x13, waiting for transfers between devices, reduce_rows(): summed = lax.psum(partial_value, 'mp')  1420 us
    psum x2, blocking collectives, on_device(): lax.psum((jnp.sum(jnp.exp(logits - peak[..., None]), axis=-1), target_loc...  393 us
    pmax x1, blocking collectives, on_device(): peak = lax.pmax(local_peak, ('segment', 'mp'))  125 us
    all_gather x1, waiting for transfers between devices, on_device(): dnorm = lax.all_gather(norm_share, ('segment', 'mp'), axis=2, tiled=True)  75.1 us
    ppermute x12, waiting for transfers between devices, shifted(): return lax.ppermute(block, axis, route)  70.4 us
    psum x1, waiting for transfers between devices, broadcast(): return lax.psum(jnp.where(mine, x, jnp.zeros_like(x)), axis)  49.1 us
  transfers between devices with their start and end apart: 30, of which 29 were waited for; matrix products, arithmetic and copies ran while one was open for 2% of the time, Pallas kernels for 0%

commit v1 on v0

--- a/solution.py
+++ b/solution.py
@@ -1,7 +1,18 @@
+import functools
 import jax
 import jax.numpy as jnp
 from jax import lax
 from jax.sharding import PartitionSpec as P
+from jax.lax import psum
+
+
+def produce_roots(in_array, axis_key, axis_id):
+    for dd in (axis_key, axis_id):
+        in_array = psum(in_array, dd)
+    return in_array
+
+
+surface_get = functools.partial(produce_roots, axis_key="mp", axis_id="segment")
 
 
 def shifted(block, axis, distance):
@@ -105,8 +116,8 @@
     local_peak = jnp.max(logits, axis=-1)
     target_local = jnp.sum(counts * logits, axis=-1)
     peak = lax.pmax(local_peak, ("segment", "mp"))
-    total, target_sum = lax.psum(
-        (jnp.sum(jnp.exp(logits - peak[..., None]), axis=-1), target_local), ("segment", "mp")
+    total, target_sum = surface_get(
+        (jnp.sum(jnp.exp(logits - peak[..., None]), axis=-1), target_local)
     )
     lse = peak + jnp.log(total)
     denom = float(micro_count * unit_count * lax.axis_size("dp"))

time: 2380 us -> 2290 us (0.962)
  blocking collectives: 518 us -> 422 us
    psum x2, blocking collectives: 393 us -> 32.6 us  [produce_roots(): in_array = psum(in_array, dd)]
    unnamed x0 -> x1, blocking collectives: none -> 264 us
where the time goes in v1:
time: 2290 us; the launch traced here: 2280 us
  waiting for transfers between devices  1670 us (73%)
  blocking collectives  422 us (18%)
  matrix products  70.2 us (3%)
  other arithmetic  53.2 us (2%)
  starting transfers between devices  28.3 us (1%)
    psum x13, waiting for transfers between devices, reduce_rows(): summed = lax.psum(partial_value, 'mp')  1420 us
    unnamed x1, blocking collectives  264 us
    pmax x1, blocking collectives, on_device(): peak = lax.pmax(local_peak, ('segment', 'mp'))  125 us
    all_gather x1, waiting for transfers between devices, on_device(): dnorm = lax.all_gather(norm_share, ('segment', 'mp'), axis=2, tiled=True)  75 us
    ppermute x12, waiting for transfers between devices, shifted(): return lax.ppermute(block, axis, route)  70.6 us
    psum x1, waiting for transfers between devices, broadcast(): return lax.psum(jnp.where(mine, x, jnp.zeros_like(x)), axis)  49.1 us
  transfers between devices with their start and end apart: 30, of which 29 were waited for; matrix products, arithmetic and copies ran while one was open for 2% of the time, Pallas kernels for 0%

profile of v1, /device:TPU:1, one launch (start us, length us, event | category | flops | bytes accessed | tf_op | source)
XLA Modules:
  0.0 2284.3 jit_solution(13711070118040740158)
XLA Ops:
  11.3 113.5 %all-reduce.19.cloned.1.call-done = f32[128,1024]{1,0:T(8,128)} async-done(((f32[128,1024]{1,0:T(8,128)}), f32[128,1024]{1,0:T(8,128)}) %all-reduce.19.cloned.1.call-update) | async-done | bytes 524304 | tf_op jit(solution)/shard_map/psum | solution.py:67
  137.0 111.0 %all-reduce.21.cloned.1.call-done = f32[128,1024]{1,0:T(8,128)} async-done(((f32[128,1024]{1,0:T(8,128)}), f32[128,1024]{1,0:T(8,128)}) %all-reduce.21.cloned.1.call-update) | async-done | bytes 524304 | tf_op jit(solution)/shard_map/psum | solution.py:67
  253.2 5.2 collective-permute-done.1
  261.9 110.8 %all-reduce.23.cloned.1.call-done = f32[128,1024]{1,0:T(8,128)} async-done(((f32[128,1024]{1,0:T(8,128)}), f32[128,1024]{1,0:T(8,128)}) %all-reduce.23.cloned.1.call-update) | async-done | bytes 524304 | tf_op jit(solution)/shard_map/psum | solution.py:67
  377.8 5.2 collective-permute-done.2
  386.5 110.8 %all-reduce.25.cloned.1.call-done = f32[128,1024]{1,0:T(8,128)} async-done(((f32[128,1024]{1,0:T(8,128)}), f32[128,1024]{1,0:T(8,128)}) %all-reduce.25.cloned.1.call-update) | async-done | bytes 524304 | tf_op jit(solution)/shard_map/psum | solution.py:67
  511.1 110.8 %all-reduce.27.cloned.1.call-done = f32[128,1024]{1,0:T(8,128)} async-done(((f32[128,1024]{1,0:T(8,128)}), f32[128,1024]{1,0:T(8,128)}) %all-reduce.27.cloned.1.call-update) | async-done | bytes 524304 | tf_op jit(solution)/shard_map/psum | solution.py:67
  635.7 110.8 %all-reduce.29.cloned.1.call-done = f32[128,1024]{1,0:T(8,128)} async-done(((f32[128,1024]{1,0:T(8,128)}), f32[128,1024]{1,0:T(8,128)}) %all-reduce.29.cloned.1.call-update) | async-done | bytes 524304 | tf_op jit(solution)/shard_map/psum | solution.py:67
  751.7 5.2 collective-permute-done.5
  760.4 110.8 %all-reduce.31.cloned.1.call-done = f32[128,1024]{1,0:T(8,128)} async-done(((f32[128,1024]{1,0:T(8,128)}), f32[128,1024]{1,0:T(8,128)}) %all-reduce.31.cloned.1.call-update) | async-done | bytes 524304 | tf_op jit(solution)/shard_map/psum | solution.py:67
  876.2 49.1 %all-reduce.33.cloned.1.call-done = bf16[4,128,1024]{2,1,0:T(8,128)(2,1)} async-done(((bf16[4,128,1024]{2,1,0:T(8,128)(2,1)}), bf16[4,128,1024]{2,1,0:T(8,128)(2,1)}) %all-reduce.33.cloned.1.call-update) | async-done | bytes 1048592 | tf_op jit(solution)/shard_map/psum | solution.py:26
  929.4 125.5 %pmax.7 = f32[4,128]{1,0:T(4,128)S(1)} all-reduce(f32[4,128]{1,0:T(4,128)S(1)} %get-tuple-element.44), channel_id=1, replica_groups=mesh['segment'=4,'mp'=16,'dp'=4] {'segment','mp'}, use_global_device_ids=true, to_apply=%region_17.18 | all-reduce | flops 512 | bytes 4096 | tf_op jit(solution)/shard_map/pmax | solution.py:118
  1057.1 26.6 %all-reduce.1 = (f32[4,128]{1,0:T(4,128)S(1)}, f32[4,128]{1,0:T(4,128)S(1)}) all-reduce(f32[4,128]{1,0:T(4,128)S(1)} %get-tuple-element.13, f32[4,128]{1,0:T(4,128)S(1)} %get-tuple-element.12), channel_id=1, replica_groups=mesh['segment'=4,'mp'=16,'dp'=4] {'mp'}, use_global_device_ids=true, to_apply=%region_24.25 | all-reduce | flops 1024 | bytes 8192 | tf_op jit(solution)/shard_map/psum | solution.py:11
  1083.7 6.0 all-reduce.2
  1095.4 264.3 %all-reduce.46 = bf16[4,128,1024]{1,0,2:T(4,128)(2,1)} all-reduce(f32[4,128,1024]{1,0,2:T(4,128)} %copy.13), channel_id=2, replica_groups=mesh['segment'=4,'mp'=16,'dp'=4] {'segment','mp'}, use_global_device_ids=true, to_apply=%region_28.29.clone | all-reduce | flops 524288 | bytes 3145728
  1361.8 75.0 %all-gather.2.cloned.1.call-done = bf16[4,128,1024]{1,0,2:T(4,128)(2,1)} async-done(((bf16[4,128,16]{1,0,2:T(4,128)(2,1)}), bf16[4,128,1024]{1,0,2:T(4,128)(2,1)}) %all-gather.2.cloned.1.call-update) | async-done | bytes 1048592 | tf_op jit(solution)/shard_map/all_gather | solution.py:135
  1444.9 106.9 %all-reduce.35.cloned.1.call-done = f32[128,1024]{1,0:T(8,128)} async-done(((f32[128,1024]{1,0:T(8,128)}), f32[128,1024]{1,0:T(8,128)}) %all-reduce.35.cloned.1.call-update) | async-done | bytes 524304 | tf_op jit(solution)/shard_map/psum | solution.py:67
  1555.9 7.3 collective-permute-done.6
  1565.9 109.8 %all-reduce.37.cloned.1.call-done = f32[128,1024]{1,0:T(8,128)} async-done(((f32[128,1024]{1,0:T(8,128)}), f32[128,1024]{1,0:T(8,128)}) %all-reduce.37.cloned.1.call-update) | async-done | bytes 524304 | tf_op jit(solution)/shard_map/psum | solution.py:67
  1680.6 6.7 collective-permute-done.7
  1691.5 109.6 %all-reduce.39.cloned.1.call-done = f32[128,1024]{1,0:T(8,128)} async-done(((f32[128,1024]{1,0:T(8,128)}), f32[128,1024]{1,0:T(8,128)}) %all-reduce.39.cloned.1.call-update) | async-done | bytes 524304 | tf_op jit(solution)/shard_map/psum | solution.py:67
  1806.1 6.7 collective-permute-done.8
  1817.0 109.8 %all-reduce.41.cloned.1.call-done = f32[128,1024]{1,0:T(8,128)} async-done(((f32[128,1024]{1,0:T(8,128)}), f32[128,1024]{1,0:T(8,128)}) %all-reduce.41.cloned.1.call-update) | async-done | bytes 524304 | tf_op jit(solution)/shard_map/psum | solution.py:67
  1931.7 6.8 collective-permute-done.9
  1942.8 109.8 %all-reduce.43.cloned.1.call-done = f32[128,1024]{1,0:T(8,128)} async-done(((f32[128,1024]{1,0:T(8,128)}), f32[128,1024]{1,0:T(8,128)}) %all-reduce.43.cloned.1.call-update) | async-done | bytes 524304 | tf_op jit(solution)/shard_map/psum | solution.py:67
  2057.6 6.7 collective-permute-done.10
  2083.5 94.8 %all-reduce.45.cloned.1.call-done = f32[128,1024]{1,0:T(8,128)} async-done(((f32[128,1024]{1,0:T(8,128)}), f32[128,1024]{1,0:T(8,128)}) %all-reduce.45.cloned.1.call-update) | async-done | bytes 524304 | tf_op jit(solution)/shard_map/psum | solution.py:67
  2182.7 7.3 collective-permute-done.11
  2190.8 6.7 multiply_add_fusion
  2209.4 7.7 multiply_add_fusion.1
  2217.8 23.4 %reduce-scatter.6.cloned.1.call-done = f32[512,256]{1,0:T(8,128)} async-done(((f32[512,1024]{1,0:T(8,128)}), f32[512,256]{1,0:T(8,128)}) %reduce-scatter.6.cloned.1.call-update) | async-done | bytes 524304 | tf_op jit(solution)/shard_map/reduce_scatter | solution.py:166
  2241.1 35.2 %reduce-scatter.4.cloned.1.call-done = f32[256,512]{1,0:T(8,128)} async-done(((f32[1024,512]{1,0:T(8,128)}), f32[256,512]{1,0:T(8,128)}) %reduce-scatter.4.cloned.1.call-update) | async-done | bytes 524304 | tf_op jit(solution)/shard_map/reduce_scatter | solution.py:165
  (285 shorter events, 170.9 us)
Async XLA Ops:
  7.2 117.6 %all-reduce.19.cloned.1.call-start = ((), (), s32[]{:S(2)}) async-start(), calls=%async_computation.3 | async-start | bytes 1048576 | tf_op jit(solution)/shard_map/psum | solution.py:67
  11.2 236.8 %all-reduce.21.cloned.1.call-start = ((), (), s32[]{:S(2)}) async-start(), calls=%async_computation.4 | async-start | bytes 1048576 | tf_op jit(solution)/shard_map/psum | solution.py:67
  126.2 8.0 collective-permute-start
  137.0 235.7 %all-reduce.23.cloned.1.call-start = ((), (), s32[]{:S(2)}) async-start(), calls=%async_computation.5 | async-start | bytes 1048576 | tf_op jit(solution)/shard_map/psum | solution.py:67
  250.1 8.3 collective-permute-start.1
  261.8 235.4 %all-reduce.25.cloned.1.call-start = ((), (), s32[]{:S(2)}) async-start(), calls=%async_computation.6 | async-start | bytes 1048576 | tf_op jit(solution)/shard_map/psum | solution.py:67
  374.7 8.3 collective-permute-start.2
  386.4 235.4 %all-reduce.27.cloned.1.call-start = ((), (), s32[]{:S(2)}) async-start(), calls=%async_computation.7 | async-start | bytes 1048576 | tf_op jit(solution)/shard_map/psum | solution.py:67
  499.3 8.3 collective-permute-start.3
  511.1 235.5 %all-reduce.29.cloned.1.call-start = ((), (), s32[]{:S(2)}) async-start(), calls=%async_computation.8 | async-start | bytes 1048576 | tf_op jit(solution)/shard_map/psum | solution.py:67
  623.9 8.3 collective-permute-start.4
  635.7 235.5 %all-reduce.31.cloned.1.call-start = ((), (), s32[]{:S(2)}) async-start(), calls=%async_computation.9 | async-start | bytes 1048576 | tf_op jit(solution)/shard_map/psum | solution.py:67
  748.6 8.3 collective-permute-start.5
  760.3 165.0 %all-reduce.33.cloned.1.call-start = ((), (), s32[]{:S(2)}) async-start(), calls=%async_computation.10 | async-start | bytes 2097152 | tf_op jit(solution)/shard_map/psum | solution.py:26
  874.2 180.6 %copy-start.55 = (s32[4,512]{1,0:T(4,128)S(1)}, s32[4,512]{1,0:T(4,128)}, u32[]{:S(2)}) copy-start(s32[4,512]{1,0:T(4,128)} %param.8) | copy-start | bytes 24580
  874.2 562.6 %all-gather.2.cloned.1.call-start = ((), (), s32[]{:S(2)}) async-start(), calls=%async_computation.11 | async-start | bytes 1064960 | tf_op jit(solution)/shard_map/all_gather | solution.py:135
  1361.0 190.8 %all-reduce.35.cloned.1.call-start = ((), (), s32[]{:S(2)}) async-start(), calls=%async_computation.12 | async-start | bytes 1048576 | tf_op jit(solution)/shard_map/psum | solution.py:67
  1361.4 192.6 %copy-start.51 = (f32[128]{0:T(128)}, f32[128]{0:T(128)S(1)}, u32[]{:S(2)}) copy-start(f32[128]{0:T(128)S(1)} %add_rsqrt_fusion.7) | copy-start | bytes 1540
  1444.9 230.8 %all-reduce.37.cloned.1.call-start = ((), (), s32[]{:S(2)}) async-start(), calls=%async_computation.13 | async-start | bytes 1048576 | tf_op jit(solution)/shard_map/psum | solution.py:67
  1554.3 9.0 collective-permute-start.6
  1565.8 235.3 %all-reduce.39.cloned.1.call-start = ((), (), s32[]{:S(2)}) async-start(), calls=%async_computation.14 | async-start | bytes 1048576 | tf_op jit(solution)/shard_map/psum | solution.py:67
  1678.3 9.0 collective-permute-start.7
  1691.5 235.4 %all-reduce.41.cloned.1.call-start = ((), (), s32[]{:S(2)}) async-start(), calls=%async_computation.15 | async-start | bytes 1048576 | tf_op jit(solution)/shard_map/psum | solution.py:67
  1803.8 9.0 collective-permute-start.8
  1817.0 235.6 %all-reduce.43.cloned.1.call-start = ((), (), s32[]{:S(2)}) async-start(), calls=%async_computation.16 | async-start | bytes 1048576 | tf_op jit(solution)/shard_map/psum | solution.py:67
  1929.5 9.0 collective-permute-start.9
  1942.7 235.6 %all-reduce.45.cloned.1.call-start = ((), (), s32[]{:S(2)}) async-start(), calls=%async_computation.17 | async-start | bytes 1048576 | tf_op jit(solution)/shard_map/psum | solution.py:67
  2055.2 9.0 collective-permute-start.10
  2068.5 149.3 %reduce-scatter.8.cloned.1.call-start = ((), (), s32[]{:S(2)}) async-start(), calls=%async_computation.20 | async-start | bytes 819200 | tf_op jit(solution)/shard_map/reduce_scatter | solution.py:167
  2071.2 170.0 %reduce-scatter.6.cloned.1.call-start = ((), (), s32[]{:S(2)}) async-start(), calls=%async_computation.19 | async-start | bytes 2621440 | tf_op jit(solution)/shard_map/reduce_scatter | solution.py:166
  2181.0 9.0 collective-permute-start.11
  2197.5 78.8 %reduce-scatter.4.cloned.1.call-start = ((), (), s32[]{:S(2)}) async-start(), calls=%async_computation.18 | async-start | bytes 2621440 | tf_op jit(solution)/shard_map/reduce_scatter | solution.py:165
  (55 other events, 548.5 us)
Sparse Core Ops, SparseCore 0:
  11.4 113.3 all-reduce.18
  137.1 110.8 all-reduce.20
  261.9 110.6 all-reduce.22
  386.6 110.6 all-reduce.24
  511.2 110.6 all-reduce.26
  635.8 110.6 all-reduce.28
  760.4 110.6 all-reduce.30
  874.4 50.9 all-reduce.32
  1361.2 75.6 all-gather.1
  1445.0 106.8 all-reduce.34
  1565.9 109.7 all-reduce.36
  1691.6 109.5 all-reduce.38
  1817.1 109.7 all-reduce.40
  1942.8 109.7 all-reduce.42
  2068.6 109.7 all-reduce.44
  2181.3 23.4 reduce-scatter.7
  2207.8 33.2 reduce-scatter.5
  2244.3 31.9 reduce-scatter.3
